TPU v7x, 32 devices: a whole 2x2x4 slice. The times are simulated.
32 devices in a mesh: dp: 4 (over x, core), seq: 8 (over z, y).
Axes of the slice: x: 2, y: 2, z: 4, core: 2. Of those that a mesh axis runs over, the one named last changes fastest.
Arguments:
- spatial_input: bfloat16 [4, 8, 64, 256], P('dp', 'seq'), may hold values from -6 to 6
- temporal_input: bfloat16 [4, 64, 8, 256], P('dp', 'seq'), may hold values from -6 to 6
- out_cotangent: bfloat16 [4, 8, 64, 256], P('dp', 'seq'), may hold values from -6 to 6
- weights: bfloat16 [2, 256, 1024], replicated, may hold values from -3 to 3
- gains: float32 [2, 256], replicated, may hold values from 0.1 to 1.9
Outputs:
- input_grad: bfloat16 [4, 8, 64, 256], P('dp', 'seq')
- weight_grads: float32 [2, 262144], P(None, ('dp', 'seq'))
- gain_grads: float32 [2, 256], replicated
All inputs are finite; a program needn't handle non-finite values.
Results may differ from a plain program's by a relative error of at most 0.023.
Values may be sent and summed in bfloat16 or wider, within the bound.
A program may use at most 64 MiB of HBM per device.

v0:
```python
from functools import partial
import math

import jax
import jax.numpy as jnp
from jax import lax
from jax.sharding import PartitionSpec as P

HEADS = 4


def one_head(head_parts, score_scale):
    query_rows, key_rows, value_rows = head_parts
    scores = (
        jnp.einsum("gqe,gke->gqk", query_rows, key_rows, preferred_element_type=jnp.float32)
        * score_scale
    )
    probs = jax.nn.softmax(scores, axis=-1).astype(jnp.bfloat16)
    return jnp.einsum("gqk,gke->gqe", probs, value_rows, preferred_element_type=jnp.float32).astype(
        jnp.bfloat16
    )


def attend_block(block_input, gain_vector, weight, head_count):
    groups, length, model_width = block_input.shape
    head_size = model_width // head_count
    mean_sq = jnp.mean(block_input * block_input, axis=-1, keepdims=True)
    normed = (block_input * lax.rsqrt(mean_sq + 1e-06) * gain_vector).astype(jnp.bfloat16)
    w_cast = weight.astype(jnp.bfloat16)
    packed = jnp.dot(
        normed.reshape(groups * length, model_width),
        w_cast[:, : 3 * model_width],
        preferred_element_type=jnp.float32,
    ).astype(jnp.bfloat16)
    packed = jnp.transpose(
        packed.reshape(groups, length, 3, head_count, head_size), (2, 3, 0, 1, 4)
    )
    head_fn = jax.checkpoint(partial(one_head, score_scale=1.0 / math.sqrt(head_size)))
    mixed_heads = lax.map(head_fn, (packed[0], packed[1], packed[2]))
    mixed_heads = jnp.transpose(mixed_heads, (1, 2, 0, 3)).reshape(groups * length, model_width)
    result = jnp.dot(mixed_heads, w_cast[:, 3 * model_width :], preferred_element_type=jnp.float32)
    return result.reshape(groups, length, model_width)


def per_device(spatial_input, temporal_input, out_cotangent, weights, gains):
    w_float = weights.astype(jnp.float32)
    block_fn = partial(attend_block, head_count=HEADS)
    sample_count = spatial_input.shape[0] * lax.axis_size("dp")
    frame_count = spatial_input.shape[1] * lax.axis_size("seq")
    patch_count = spatial_input.shape[2]
    grad_factor = 1.0 / math.sqrt(sample_count * frame_count * patch_count)
    patch_major = jnp.swapaxes(out_cotangent[0], 0, 1)
    temporal_cot = lax.all_to_all(
        patch_major, "seq", split_axis=0, concat_axis=1, tiled=True
    ).astype(jnp.float32)
    unused_t, pullback_t = jax.vjp(
        block_fn, temporal_input[0].astype(jnp.float32), gains[1], w_float[1]
    )
    grad_ut, grad_gt, grad_wt = pullback_t(temporal_cot)
    temporal_term = (grad_wt * grad_factor).reshape(1, -1)
    mid_grad = (temporal_cot + grad_ut).astype(jnp.bfloat16)
    frame_back = lax.all_to_all(mid_grad, "seq", split_axis=1, concat_axis=0, tiled=True)
    spatial_cot = jnp.swapaxes(frame_back, 0, 1).astype(jnp.float32)
    unused_s, pullback_s = jax.vjp(
        block_fn, spatial_input[0].astype(jnp.float32), gains[0], w_float[0]
    )
    grad_us, grad_gs, grad_ws = pullback_s(spatial_cot)
    input_grad = (spatial_cot + grad_us).astype(jnp.bfloat16)[None]
    spatial_term = (grad_ws * grad_factor).reshape(1, -1)
    both_terms = jnp.concatenate([spatial_term, temporal_term], axis=0)
    grid_terms = both_terms.reshape(2, lax.axis_size("dp"), lax.axis_size("seq"), -1)
    over_frames = lax.psum_scatter(
        grid_terms.astype(jnp.bfloat16), "seq", scatter_dimension=2, tiled=True
    ).astype(jnp.float32)
    over_frames = over_frames.reshape(2, lax.axis_size("dp"), -1)
    weight_grads = (
        lax.psum_scatter(over_frames.astype(jnp.bfloat16), "dp", scatter_dimension=1, tiled=True)
        .astype(jnp.float32)
        .reshape(2, -1)
    )
    gain_grads = lax.psum(jnp.stack([grad_gs, grad_gt]) * grad_factor, ("dp", "seq"))
    return (input_grad, weight_grads, gain_grads)


def solution(mesh):
    return jax.shard_map(
        per_device,
        mesh=mesh,
        in_specs=(
            P("dp", "seq", None, None),
            P("dp", "seq", None, None),
            P("dp", "seq", None, None),
            P(),
            P(),
        ),
        out_specs=(P("dp", "seq", None, None), P(None, ("dp", "seq")), P()),
        check_vma=False,
    )
```

profile of v0, /device:TPU:0, one launch (start us, length us, event | category | flops | bytes accessed | tf_op | source)
XLA Modules:
  0.0 179.6 jit_solution(7019148246470243943)
XLA Ops:
  7.2 0.5 broadcast.288
  7.7 1.4 reduce.34
  9.1 0.6 reshape.395
  9.7 7.4 %all-to-all-start = ((bf16[8,2,1024]{2,1,0:T(2,128)(2,1)}), bf16[8,2,1024]{2,1,0:T(2,128)(2,1)S(1)}, u32[]{:S(2)}, u32[]{:S(2)}) async-start(bf16[8,2,1024]{2,1,0:T(2,128)(2,1)} %reshape.395), calls=%async_computation | async-start | bytes 65536 | tf_op jit(solution)/shard_map/all_to_all | solution.py:53
  17.3 0.7 copy-done.1
  18.1 0.6 copy-done.2
  18.9 1.3 slice_bitcast_fusion.1
  20.6 2.0 %while.59 = (s32[]{:T(128)}, bf16[4,8,8,64]{3,2,1,0:T(8,128)(2,1)S(1)}, bf16[4,8,8,64]{3,2,1,0:T(8,128)(2,1)S(1)}, bf16[4,8,8,64]{3,2,1,0:T(8,128)(2,1)S(1)}, bf16[4,8,8,64]{3,2,1,0:T(8,128)(2,1)S(1)}, /*index=5*/s32[]{:T(128)}) while((s32[]{:T(128)}, bf16[4,8,8,64]{3,2,1,0:T(8,128)(2,1)S(1)}, bf16[4,8,8,64]{3,2,1,0:T(8,128)(2,1)S(1)}, ...), condition=%wide.region_21.22_spmd, body=%wide.region_18.0_spmd.sunk | while | flops 204368 | bytes 105805 | solution.py:39
  20.8 0.3 fusion.234
  21.3 0.3 fusion.234
  21.8 0.3 fusion.234
  22.3 0.3 fusion.234
  23.1 1.6 while.58
  25.6 4.9 %while.56 = (s32[]{:T(128)}, bf16[4,8,8,64]{3,2,1,0:T(8,128)(2,1)S(1)}, bf16[4,8,8,64]{3,2,1,0:T(8,128)(2,1)S(1)}, bf16[4,8,8,64]{3,2,1,0:T(8,128)(2,1)S(1)}, bf...) while((s32[]{:T(128)}, ...), condition=%wide.region_5.6_spmd, body=%wide.region_1.5_spmd.sunk | while | flops 549215 | bytes 388997 | solution.py:39
  25.9 0.3 fusion.215
  26.2 0.3 fusion.214
  26.5 0.3 fusion.213
  27.2 0.3 fusion.215
  27.4 0.3 fusion.214
  27.7 0.3 fusion.213
  28.4 0.3 fusion.215
  28.6 0.3 fusion.214
  28.9 0.3 fusion.213
  29.6 0.3 fusion.215
  29.9 0.3 fusion.214
  30.1 0.3 fusion.213
  30.9 0.3 fusion.84
  31.3 0.7 fusion.99
  32.0 6.0 %all-to-all-start.1 = ((bf16[8,8,256]{2,0,1:T(8,128)(2,1)}), bf16[8,8,256]{2,0,1:T(8,128)(2,1)S(1)}, u32[]{:S(2)}, u32[]{:S(2)}) async-start(bf16[8,8,256]{2,0,1:T(8,128)(2,1)} %fusion.99), calls=%async_computation.1 | async-start | bytes 65536 | tf_op jit(solution)/shard_map/all_to_all | solution.py:62
  38.2 0.3 convolution_convert_fusion.10
  38.6 0.2 concatenate.10
  38.9 0.4 copy.103
  39.3 5.4 %all-to-all-done.1 = bf16[8,8,256]{2,0,1:T(8,128)(2,1)S(1)} async-done(((bf16[8,8,256]{2,0,1:T(8,128)(2,1)}), bf16[8,8,256]{2,0,1:T(8,128)(2,1)S(1)}, u32[]{:S(2)}, u32[]{:S(2)}) %all-to-all-start.1) | async-done | bytes 32800 | tf_op jit(solution)/shard_map/all_to_all | solution.py:62
  45.0 4.7 %while.57 = (s32[]{:T(128)}, bf16[4,1,64,64]{2,3,0,1:T(8,128)(2,1)S(1)}, bf16[4,1,64,64]{2,3,0,1:T(8,128)(2,1)S(1)}, bf16[4,1,64,64]{2,3,1,0:T(8,128)(2,1)S(1)},...) while((s32[]{:T(128)}, ...), condition=%wide.region_12.13_spmd, body=%wide.region_8.12_spmd.sunk | while | flops 2727939 | bytes 431237 | solution.py:39
  49.8 0.4 convolution_convert_fusion.11
  50.4 0.2 concatenate.9
  50.7 0.4 copy.102
  51.1 1.7 pad_maximum_fusion
  52.9 0.6 copy-done.4
  53.6 0.6 dynamic-slice.2
  54.2 0.6 dynamic-slice
  54.8 0.4 fusion.97
  55.2 0.7 fusion.117
  55.9 72.8 %all-reduce.15.cloned.1.call-done = bf16[2,4,8,8192]{3,1,0,2:T(4,128)(2,1)} async-done(((bf16[2,4,8,8192]{3,1,0,2:T(4,128)(2,1)}), bf16[2,4,8,8192]{3,1,0,2:T(4,128)(2,1)}) %all-reduce.15.cloned.1.call-update) | async-done | bytes 1048592
  128.7 1.6 dynamic-slice_bitcast_fusion.8
  130.3 0.8 copy.104
  131.1 39.6 %psum.7 = f32[2,256]{1,0:T(2,128)} all-reduce(f32[2,256]{1,0:T(2,128)S(1)} %maximum_multiply_fusion), channel_id=1, replica_groups=mesh['dp'=4,'seq'=8] {'dp','seq'}, use_global_device_ids=true, to_apply=%region_26.27 | all-reduce | flops 512 | bytes 4096 | tf_op jit(solution)/shard_map/psum | solution.py:81
  170.7 2.0 %bitcast_convert_fusion = f32[2,8192]{1,0:T(2,128)} fusion(bf16[2,4,8192]{2,0,1:T(2,128)(2,1)} %all-reduce.17.cloned.1.call-done, u32[]{:T(128)} %bitcast.79), kind=kLoop, calls=%fused_computation.171 | loop fusion | flops 16384 | bytes 98308 | tf_op jit(solution)/shard_map/reshape | solution.py:79
  (158 shorter events, 11.6 us)
Async XLA Ops:
  9.7 7.4 %copy-start = (bf16[1,8,8,256]{3,2,1,0:T(8,128)(2,1)S(1)}, bf16[1,8,8,256]{3,2,1,0:T(8,128)(2,1)}, u32[]{:S(2)}) copy-start(bf16[1,8,8,256]{3,2,1,0:T(8,128)(2,1)} %param.14) | copy-start | bytes 98308
  9.7 15.4 %all-to-all-start = ((bf16[8,2,1024]{2,1,0:T(2,128)(2,1)}), bf16[8,2,1024]{2,1,0:T(2,128)(2,1)S(1)}, u32[]{:S(2)}, u32[]{:S(2)}) async-start(bf16[8,2,1024]{2,1,0:T(2,128)(2,1)} %reshape.395), calls=%async_computation | async-start | bytes 65536 | tf_op jit(solution)/shard_map/all_to_all | solution.py:53
  17.3 0.8 copy-start.1
  18.0 0.7 copy-start.2
  32.0 12.7 %all-to-all-start.1 = ((bf16[8,8,256]{2,0,1:T(8,128)(2,1)}), bf16[8,8,256]{2,0,1:T(8,128)(2,1)S(1)}, u32[]{:S(2)}, u32[]{:S(2)}) async-start(bf16[8,8,256]{2,0,1:T(8,128)(2,1)} %fusion.99), calls=%async_computation.1 | async-start | bytes 65536 | tf_op jit(solution)/shard_map/all_to_all | solution.py:62
  38.0 90.8 %all-reduce.15.cloned.1.call-start = ((), (), s32[]{:S(2)}) async-start(), calls=%async_computation.2 | async-start | bytes 2097152
  52.9 117.9 %all-reduce.17.cloned.1.call-start = ((), (), s32[]{:S(2)}) async-start(), calls=%async_computation.3 | async-start | bytes 262144
  52.9 0.7 copy-start.4
  53.6 0.7 copy-start.3
Sparse Core Ops, SparseCore 0:
  53.0 75.6 all-reduce.14
  131.2 31.3 all-reduce.16
where the time goes:
time: 180 us
  waiting for transfers between devices  78.2 us (43%)
  blocking collectives  39.6 us (22%)
  between operations  14.4 us (8%)
  matrix products  13.7 us (8%)
  starting transfers between devices  13.5 us (8%)
  local copies, waits for them, and re-layouts  12 us (7%)
  other arithmetic  7.74 us (4%)
    unnamed x4, waiting for transfers between devices  72.8 us
    psum x1, blocking collectives, per_device(): lax.psum(jnp.stack([grad_gs, grad_gt]) * grad_factor, ('dp', 'seq'))  39.6 us
    all_to_all x1, starting transfers between devices, per_device(): lax.all_to_all(patch_major, 'seq', split_axis=0, concat_axis=1, tiled=True)  7.44 us
    all_to_all x1, starting transfers between devices, per_device(): lax.all_to_all(mid_grad, 'seq', split_axis=1, concat_axis=0, tiled=True)  5.99 us
    all_to_all x1, waiting for transfers between devices, per_device(): lax.all_to_all(mid_grad, 'seq', split_axis=1, concat_axis=0, tiled=True)  5.36 us
    dot_general x24, matrix products, one_head(): jnp.einsum('gqk,gke->gqe', probs, value_rows, preferred_element_type=jnp....  5.11 us
    dot_general x24, matrix products, one_head(): jnp.einsum('gqe,gke->gqk', query_rows, key_rows, preferred_element_type=j...  4.94 us
    unnamed x15, local copies, waits for them, and re-layouts  3.85 us
  transfers between devices with their start and end apart: 4, of which 2 were waited for; matrix products, arithmetic and copies ran while one was open for 6% of the time, Pallas kernels for 0%

commit v1 on v0

v1 whole, which is shorter than its diff:
```python
from functools import partial
import math

import jax
import jax.numpy as jnp
from jax import lax
from jax.experimental import pallas as pl
from jax.experimental.pallas import tpu as pltpu
from jax.sharding import PartitionSpec as P

HEADS = 4
F32 = jnp.float32
BF16 = jnp.bfloat16
MESH = pl.DeviceIdType.MESH


def dot(a, b, ca, cb):
    return lax.dot_general(a, b, (((ca,), (cb,)), ((), ())), preferred_element_type=F32)


def fold(x, parts):
    rows, width = x.shape
    x = x.reshape(parts, rows // parts, width)
    return jnp.concatenate([x[:, :, : width // 2], x[:, :, width // 2 :]], axis=1)


def unfold(x):
    parts, rows, half = x.shape
    x = jnp.concatenate([x[:, : rows // 2], x[:, rows // 2 :]], axis=2)
    return x.reshape(parts * (rows // 2), 2 * half)


def head_masks(rows, width):
    lane = lax.broadcasted_iota(jnp.int32, (rows, width), 1)
    size = width // HEADS
    return [(lane >= h * size) & (lane < (h + 1) * size) for h in range(HEADS)]


def spread(x, masks):
    zero = jnp.zeros_like(x)
    return jnp.concatenate([jnp.where(m, x, zero) for m in masks], axis=0)


def gather_heads(x, masks):
    rows = x.shape[0] // HEADS
    out = x[:rows]
    for h in range(1, HEADS):
        out = jnp.where(masks[h], x[h * rows : (h + 1) * rows], out)
    return out


def forward(u, gain, w_ref, block, same_group):
    rows, width = u.shape
    masks = head_masks(rows, width)
    scale = 1.0 / math.sqrt(width // HEADS)
    inv = lax.rsqrt(jnp.mean(u * u, axis=-1, keepdims=True) + 1e-06)
    unit = u * inv
    normed = (unit * gain).astype(BF16)
    packed = dot(normed, w_ref[block, :, : 3 * width], 1, 0)
    q, k, v = (packed[:, i * width : (i + 1) * width] for i in range(3))
    qs = spread(q, masks).astype(BF16)
    k = k.astype(BF16)
    v = v.astype(BF16)
    scores = dot(qs, k, 1, 1) * scale
    if same_group is not None:
        scores = jnp.where(same_group, scores, -1e30)
    e = jnp.exp(scores - jnp.max(scores, axis=-1, keepdims=True))
    probs = e / jnp.sum(e, axis=-1, keepdims=True)
    pb = probs.astype(BF16)
    mixed = gather_heads(dot(pb, v, 1, 0), masks).astype(BF16)
    return dict(unit=unit, inv=inv, normed=normed, qs=qs, k=k, v=v, probs=probs, pb=pb, mixed=mixed)


def backward_heads(cot, s, w_ref, block):
    rows, width = cot.shape
    masks = head_masks(rows, width)
    scale = 1.0 / math.sqrt(width // HEADS)
    dmixed = dot(cot, w_ref[block, :, 3 * width :], 1, 1)
    dms = spread(dmixed, masks).astype(BF16)
    dprobs = dot(dms, s["v"], 1, 1).astype(BF16).astype(F32)
    inner = jnp.sum(dprobs * s["probs"], axis=-1, keepdims=True)
    dscores = (s["probs"] * (dprobs - inner) * scale).astype(BF16)
    dq = gather_heads(dot(dscores, s["k"], 1, 0), masks)
    dk = dot(dscores, s["qs"], 0, 0)
    dv = dot(s["pb"], dms, 0, 0)
    return dq.astype(BF16), dk.astype(BF16), dv.astype(BF16)


def backward_input(dpacked, s, gain, w_ref, block):
    width = gain.shape[1]
    dn = dot(dpacked, w_ref[block, :, : 3 * width], 1, 1).astype(BF16).astype(F32)
    unit = s["unit"]
    dgain = jnp.sum(dn * unit, axis=0, keepdims=True)
    t = dn * gain
    du = s["inv"] * (t - unit * jnp.mean(unit * t, axis=-1, keepdims=True))
    return du, dgain


def weight_halves(cot, dq, dk, dv, s):
    n = s["normed"]
    left = dot(n, jnp.concatenate([dq, dk], axis=1), 0, 0)
    right = jnp.concatenate([dot(n, dv, 0, 0), dot(s["mixed"], cot, 0, 0)], axis=1)
    return left, right


def kernel(ndp, nseq, fused, factor, *refs):
    sp_ref, tp_ref, cot_ref, w_ref, g_ref = refs[:5]
    ig_ref, wg_ref, gg_ref = refs[5:8]
    csend, crecv, msend, mrecv, x_send, x_recv = refs[8:14]
    dp, seq = lax.axis_index("dp"), lax.axis_index("seq")
    rows, width = cot_ref.shape
    per = rows // nseq
    nfar = ndp // 2 * nseq
    core = lax.rem(dp, 2)
    partner = (dp + 1 - 2 * core, seq)
    me = lax.div(dp, 2) * nseq + seq

    def far(i):
        other = lax.rem(me + i, nfar)
        x = lax.div(other, nseq)
        return other, (2 * x + core, other - x * nseq)

    def near(i):
        other = lax.rem(seq + i, nseq)
        return other, (dp, other)

    barrier = pltpu.get_barrier_semaphore()
    if fused:
        pl.semaphore_signal(barrier, inc=1, device_id=partner, device_id_type=MESH)

    peer, npeer = (far, nfar) if fused else (near, nseq)

    @pl.loop(1, npeer)
    def _(i):
        pl.semaphore_signal(barrier, inc=1, device_id=peer(i)[1], device_id_type=MESH)

    def exchange(level, send, recv):
        def copy(i, slot):
            other, device = near(i)
            return pltpu.make_async_remote_copy(
                src_ref=send.at[other],
                dst_ref=recv.at[slot(other)],
                send_sem=x_send.at[level, other],
                recv_sem=x_recv.at[level, slot(other)],
                device_id=device,
                device_id_type=MESH,
            )

        def start():
            @pl.loop(1, nseq)
            def _(i):
                copy(i, lambda other: seq).start()

        def arrive():
            @pl.loop(1, nseq)
            def _(i):
                copy(i, lambda other: other).wait_recv()

        def finish():
            @pl.loop(1, nseq)
            def _(i):
                copy(i, lambda other: seq).wait_send()

        return start, arrive, finish

    c_start, c_arrive, c_finish = exchange(0, csend, crecv)
    m_start, m_arrive, m_finish = exchange(1, msend, mrecv)

    csend[...] = fold(cot_ref[...].astype(F32), nseq).astype(BF16)
    crecv[seq] = csend[seq]

    frames = rows // per
    at = lax.broadcasted_iota(jnp.int32, (rows, rows), 0)
    frm = lax.broadcasted_iota(jnp.int32, (rows, rows), 1)
    pick = (frm == lax.rem(at, per) * frames + lax.div(at, per)).astype(F32).astype(BF16)
    ut = dot(pick, tp_ref[...], 1, 0)
    ri = lax.broadcasted_iota(jnp.int32, (HEADS * rows, rows), 0)
    ci = lax.broadcasted_iota(jnp.int32, (HEADS * rows, rows), 1)
    same = lax.rem(ri, per) == lax.rem(ci, per)
    g_t, g_s = g_ref[1:2, :], g_ref[0:1, :]
    st = forward(ut, g_t, w_ref, 1, same)

    pl.semaphore_wait(barrier, npeer if fused else npeer - 1)
    c_start()
    ss = forward(sp_ref[...].astype(F32), g_s, w_ref, 0, None)
    c_arrive()

    if fused:
        part, arecv, bsend, brecv, gown, garecv, gbsend, gbrecv = refs[14:22]
        a_send, a_recv, b_send, b_recv = refs[22:26]
        chunk = part.shape[3]

        def near_copy(level, src, dst):
            return pltpu.make_async_remote_copy(
                src_ref=src,
                dst_ref=dst,
                send_sem=a_send.at[level],
                recv_sem=a_recv.at[level],
                device_id=partner,
                device_id_type=MESH,
            )

        a_copies = [near_copy(b, part.at[b, 1 - core], arecv.at[b]) for b in range(2)]
        a_copies.append(near_copy(2, gown, garecv))

        def far_copy(level, i, sending):
            other, device = far(i)
            slot = me if sending else other
            if level == 2:
                src, dst = gbsend, gbrecv.at[slot]
            else:
                src, dst = bsend.at[level, other], brecv.at[level, slot]
            return pltpu.make_async_remote_copy(
                src_ref=src,
                dst_ref=dst,
                send_sem=b_send.at[level, other],
                recv_sem=b_recv.at[level, slot],
                device_id=device,
                device_id_type=MESH,
            )

        def put_weights(b, left, right):
            both = jnp.concatenate(
                [left.reshape(2 * nfar, chunk // 2, -1), right.reshape(2 * nfar, chunk // 2, -1)],
                axis=1,
            ).astype(BF16)
            both = both.reshape(ndp // 2, 2, nseq, chunk, -1)
            for c in range(2):
                part[b, c] = both[:, c].reshape(nfar, chunk, -1)
            a_copies[b].start()

        def far_start(b):
            a_copies[b].wait_recv()
            total = part[b, core].astype(F32) + arecv[b].astype(F32)
            bsend[b] = total.astype(BF16)
            brecv[b, me] = bsend[b, me]

            @pl.loop(1, nfar)
            def _(i):
                far_copy(b, i, True).start()

        def far_end(b):
            @pl.loop(1, nfar)
            def _(i):
                far_copy(b, i, False).wait_recv()

            total = jnp.sum(brecv[b].astype(F32), axis=0) * factor
            r = chunk // 2
            half = total.shape[1]
            for i in range(r):
                wg_ref[b : b + 1, 2 * i * half : (2 * i + 1) * half] = total[i : i + 1]
                wg_ref[b : b + 1, (2 * i + 1) * half : (2 * i + 2) * half] = total[r + i : r + i + 1]
    else:

        def put_weights(b, left, right):
            w = left.shape[1]
            wg_ref[b, :, :w] = (left * factor).astype(BF16)
            wg_ref[b, :, w:] = (right * factor).astype(BF16)

    cot_t = unfold(crecv[...].astype(F32))
    cot_tb = cot_t.astype(BF16)
    dq, dk, dv = backward_heads(cot_tb, st, w_ref, 1)
    du, dg_t = backward_input(jnp.concatenate([dq, dk, dv], axis=1), st, g_t, w_ref, 1)
    msend[...] = fold(cot_t + du, nseq).astype(BF16)
    mrecv[seq] = msend[seq]
    m_start()
    put_weights(1, *weight_halves(cot_tb, dq, dk, dv, st))

    m_arrive()
    cot_s = unfold(mrecv[...].astype(F32))
    cot_sb = cot_s.astype(BF16)
    if fused:
        far_start(1)
    dq, dk, dv = backward_heads(cot_sb, ss, w_ref, 0)
    put_weights(0, *weight_halves(cot_sb, dq, dk, dv, ss))
    du, dg_s = backward_input(jnp.concatenate([dq, dk, dv], axis=1), ss, g_s, w_ref, 0)
    ig_ref[...] = (cot_s + du).astype(BF16)

    if fused:
        gown[...] = jnp.zeros_like(gown)
        gown[0:1, :] = dg_s
        gown[1:2, :] = dg_t
        a_copies[2].start()
        far_start(0)
        a_copies[2].wait_recv()
        gbsend[...] = gown[...] + garecv[...]
        gbrecv[me] = gbsend[...]

        @pl.loop(1, nfar)
        def _(i):
            far_copy(2, i, True).start()

        far_end(1)
        far_end(0)

        @pl.loop(1, nfar)
        def _(i):
            far_copy(2, i, False).wait_recv()

        gg_ref[...] = jnp.sum(gbrecv[...], axis=0)[0:2] * factor
        for c in a_copies:
            c.wait_send()
        for level in range(3):

            @pl.loop(1, nfar)
            def _(i):
                far_copy(level, i, True).wait_send()
    else:
        gg_ref[0:1, :] = dg_s * factor
        gg_ref[1:2, :] = dg_t * factor
    c_finish()
    m_finish()


def per_device(spatial_input, temporal_input, out_cotangent, weights, gains):
    ndp, nseq = lax.axis_size("dp"), lax.axis_size("seq")
    width = spatial_input.shape[-1]
    rows = spatial_input.shape[1] * spatial_input.shape[2]
    factor = 1.0 / math.sqrt(spatial_input.shape[0] * ndp * nseq * rows)
    per = rows // nseq
    wide = weights.shape[2]
    chunk_rows = width // (ndp * nseq)
    fused = ndp % 2 == 0 and chunk_rows * ndp * nseq == width and chunk_rows % 8 == 0
    nfar = ndp // 2 * nseq
    message = pltpu.VMEM((nseq, 2 * per, width // 2), BF16)
    scratch = [message] * 4 + [pltpu.SemaphoreType.DMA((2, nseq))] * 2
    if fused:
        block = (2 * chunk_rows, wide // 2)
        scratch += [
            pltpu.VMEM((2, 2, nfar) + block, BF16),
            pltpu.VMEM((2, nfar) + block, BF16),
            pltpu.VMEM((2, nfar) + block, BF16),
            pltpu.VMEM((2, nfar) + block, BF16),
            pltpu.VMEM((8, width), F32),
            pltpu.VMEM((8, width), F32),
            pltpu.VMEM((8, width), F32),
            pltpu.VMEM((nfar, 8, width), F32),
            pltpu.SemaphoreType.DMA((3,)),
            pltpu.SemaphoreType.DMA((3,)),
            pltpu.SemaphoreType.DMA((3, nfar)),
            pltpu.SemaphoreType.DMA((3, nfar)),
        ]
        wg_shape = jax.ShapeDtypeStruct((2, chunk_rows * wide), F32)
    else:
        wg_shape = jax.ShapeDtypeStruct((2, width, wide), BF16)
    vmem = pl.BlockSpec(memory_space=pltpu.VMEM)
    input_grad, weight_grads, gain_grads = pl.pallas_call(
        partial(kernel, ndp, nseq, fused, factor),
        out_shape=(
            jax.ShapeDtypeStruct((rows, width), BF16),
            wg_shape,
            jax.ShapeDtypeStruct((2, width), F32),
        ),
        in_specs=[vmem] * 5,
        out_specs=(vmem,) * 3,
        scratch_shapes=scratch,
        compiler_params=pltpu.CompilerParams(
            collective_id=0, has_side_effects=True, vmem_limit_bytes=48 * 1024 * 1024
        ),
    )(
        spatial_input.reshape(rows, width),
        temporal_input.reshape(rows, width),
        out_cotangent.reshape(rows, width),
        weights,
        gains,
    )
    if not fused:
        grid = weight_grads.reshape(2, ndp, nseq, -1)
        over = lax.psum_scatter(grid, "seq", scatter_dimension=2, tiled=True)
        over = lax.psum_scatter(
            over.reshape(2, ndp, -1), "dp", scatter_dimension=1, tiled=True
        )
        weight_grads = over.astype(F32).reshape(2, -1)
        gain_grads = lax.psum(gain_grads, ("dp", "seq"))
    return input_grad.reshape(spatial_input.shape), weight_grads, gain_grads


def solution(mesh):
    return jax.shard_map(
        per_device,
        mesh=mesh,
        in_specs=(
            P("dp", "seq", None, None),
            P("dp", "seq", None, None),
            P("dp", "seq", None, None),
            P(),
            P(),
        ),
        out_specs=(P("dp", "seq", None, None), P(None, ("dp", "seq")), P()),
        check_vma=False,
    )
```

time: 180 us -> 39.2 us (0.22)
  waiting for transfers between devices: 78.2 us -> 0 us
  blocking collectives: 39.6 us -> 0 us
  Pallas kernels: 0 us -> 32.2 us
  between operations: 14.4 us -> 0.65 us
  matrix products: 13.7 us -> 0 us
  starting transfers between devices: 13.5 us -> 0 us
  other arithmetic: 7.74 us -> 0 us
  local copies, waits for them, and re-layouts: 12 us -> 5.99 us
    unnamed x4 -> x0, waiting for transfers between devices: 72.8 us -> none
    psum x1 -> x0, blocking collectives: 39.6 us -> none  [per_device(): lax.psum(jnp.stack([grad_gs, grad_gt]) * grad_factor, ('dp', 'seq'))]
    pallas_call x0 -> x1, Pallas kernels: none -> 32.2 us  [per_device(): pl.pallas_call(partial(kernel, ndp, nseq, fused, factor), out_shape=(jax....]
    all_to_all x2 -> x0, starting transfers between devices: 13.4 us -> none  [the longest x1 7.44 us: per_device(): lax.all_to_all(patch_major, 'seq', split_axis=0, concat_axis=1, tiled=True)]
    dot_general x58 -> x0, matrix products: 12.5 us -> none  [the longest x24 5.11 us: one_head(): jnp.einsum('gqk,gke->gqe', probs, value_rows, preferred_element_type=jnp....]
    all_to_all x2 -> x0, waiting for transfers between devices: 5.36 us -> none  [the longest x1 5.36 us: per_device(): lax.all_to_all(mid_grad, 'seq', split_axis=1, concat_axis=0, tiled=True)]
    convert_element_type x3 -> x0, local copies, waits for them, and re-layouts: 3.66 us -> none  [the longest x2 2.38 us: per_device(): over_frames.astype(jnp.bfloat16)]
    unnamed x15 -> x13, local copies, waits for them, and re-layouts: 3.85 us -> 5.99 us
  transfers between devices with their start and end apart: 4 -> 0, of which waited for: 2 -> 0; matrix products, arithmetic and copies ran while one was open for 6% -> 0% of each run, Pallas kernels for 0% -> 0%
where the time goes in v1:
time: 39.2 us; the launch traced here: 38.8 us
  Pallas kernels  32.2 us (82%)
  local copies, waits for them, and re-layouts  5.99 us (15%)
  between operations  0.65 us (2%)
    pallas_call x1, Pallas kernels, per_device(): pl.pallas_call(partial(kernel, ndp, nseq, fused, factor), out_shape=(jax....  32.2 us
    unnamed x13, local copies, waits for them, and re-layouts  5.99 us

profile of v1, /device:TPU:0, one launch (start us, length us, event | category | flops | bytes accessed | tf_op | source)
XLA Modules:
  0.0 38.8 jit_solution(12402879816314671662)
XLA Ops:
  0.6 0.0 copy-start.4
  0.6 0.7 %copy-done.4 = f32[2,256]{1,0:T(2,128)S(1)} copy-done((f32[2,256]{1,0:T(2,128)S(1)}, f32[2,256]{1,0:T(2,128)}, u32[]{:S(2)}) %copy-start.4) | copy-done | bytes 2072
  1.3 0.0 copy-start
  1.3 1.2 %copy-done = bf16[2,256,1024]{2,1,0:T(8,128)(2,1)S(1)} copy-done((bf16[2,256,1024]{2,1,0:T(8,128)(2,1)S(1)}, bf16[2,256,1024]{2,1,0:T(8,128)(2,1)}, u32[]{:S(2)}) %copy-start) | copy-done | bytes 1048600
  2.5 0.0 copy-start.1
  2.5 0.8 %copy-done.1 = bf16[1,1,64,256]{3,2,1,0:T(8,128)(2,1)S(1)} copy-done((bf16[1,1,64,256]{3,2,1,0:T(8,128)(2,1)S(1)}, bf16[1,1,64,256]{3,2,1,0:T(8,128)(2,1)}, u32[]{:S(2)}) %copy-start.1) | copy-done | bytes 32792
  3.3 0.0 copy-start.2
  3.3 0.8 %copy-done.2 = bf16[1,8,8,256]{3,2,1,0:T(8,128)(2,1)S(1)} copy-done((bf16[1,8,8,256]{3,2,1,0:T(8,128)(2,1)S(1)}, bf16[1,8,8,256]{3,2,1,0:T(8,128)(2,1)}, u32[]{:S(2)}) %copy-start.2) | copy-done | bytes 32792
  4.1 0.0 copy-start.3
  4.1 0.8 %copy-done.3 = bf16[1,1,64,256]{3,2,1,0:T(8,128)(2,1)S(1)} copy-done((bf16[1,1,64,256]{3,2,1,0:T(8,128)(2,1)S(1)}, bf16[1,1,64,256]{3,2,1,0:T(8,128)(2,1)}, u32[]{:S(2)}) %copy-start.3) | copy-done | bytes 32792
  4.8 32.2 %shard_map.76 = (bf16[64,256]{1,0:T(8,128)(2,1)S(1)}, f32[2,8192]{1,0:T(2,128)S(1)}, f32[2,256]{1,0:T(2,128)S(1)}) custom-call(bf16[64,256]{1,0:T(8,128)(2,1)S(1)} %bitcast.4, bf16[64,256]{1,0:T(8,128)(2,1)S(1)} %bitcast.5, bf16[64,256]{1,0:T(8,128)(2,1)S(1)} %bitcast.6, bf16[2,256,1024]{2,1,0:T(8,128)(2,1)S(1)} %copy-done, f32[2,256]{1,0:T(2,128)S(1)} %copy-done.4), custom_call_target="tpu_custom_call" | custom-call | tf_op jit(solution)/shard_map/pallas_call | solution.py:347
  37.0 0.6 %copy.11 = bf16[1,1,64,256]{3,2,1,0:T(8,128)(2,1)} copy(bf16[1,1,64,256]{3,2,1,0:T(8,128)(2,1)S(1)} %bitcast.7) | data formatting | bytes 65536
  37.6 0.6 %copy.12 = f32[2,8192]{1,0:T(2,128)} copy(f32[2,8192]{1,0:T(2,128)S(1)} %get-tuple-element.13) | data formatting | bytes 131072
  38.2 0.6 %copy.13 = f32[2,256]{1,0:T(2,128)} copy(f32[2,256]{1,0:T(2,128)S(1)} %get-tuple-element.14) | data formatting | bytes 4096
Async XLA Ops:
  0.6 0.7 %copy-start.4 = (f32[2,256]{1,0:T(2,128)S(1)}, f32[2,256]{1,0:T(2,128)}, u32[]{:S(2)}) copy-start(f32[2,256]{1,0:T(2,128)} %refs_4_.1) | copy-start | bytes 6148
  1.3 1.2 %copy-start = (bf16[2,256,1024]{2,1,0:T(8,128)(2,1)S(1)}, bf16[2,256,1024]{2,1,0:T(8,128)(2,1)}, u32[]{:S(2)}) copy-start(bf16[2,256,1024]{2,1,0:T(8,128)(2,1)} %refs_3_.1) | copy-start | bytes 3145732
  2.5 0.8 %copy-start.1 = (bf16[1,1,64,256]{3,2,1,0:T(8,128)(2,1)S(1)}, bf16[1,1,64,256]{3,2,1,0:T(8,128)(2,1)}, u32[]{:S(2)}) copy-start(bf16[1,1,64,256]{3,2,1,0:T(8,128)(2,1)} %param.5) | copy-start | bytes 98308
  3.3 0.8 %copy-start.2 = (bf16[1,8,8,256]{3,2,1,0:T(8,128)(2,1)S(1)}, bf16[1,8,8,256]{3,2,1,0:T(8,128)(2,1)}, u32[]{:S(2)}) copy-start(bf16[1,8,8,256]{3,2,1,0:T(8,128)(2,1)} %param.6) | copy-start | bytes 98308
  4.1 0.8 %copy-start.3 = (bf16[1,1,64,256]{3,2,1,0:T(8,128)(2,1)S(1)}, bf16[1,1,64,256]{3,2,1,0:T(8,128)(2,1)}, u32[]{:S(2)}) copy-start(bf16[1,1,64,256]{3,2,1,0:T(8,128)(2,1)} %param.7) | copy-start | bytes 98308

commit v2 on v1

--- a/solution.py
+++ b/solution.py
@@ -104,9 +104,21 @@
 
 
 def kernel(ndp, nseq, fused, factor, *refs):
-    sp_ref, tp_ref, cot_ref, w_ref, g_ref = refs[:5]
     ig_ref, wg_ref, gg_ref = refs[5:8]
-    csend, crecv, msend, mrecv, x_send, x_recv = refs[8:14]
+    sp_ref, tp_ref, cot_ref, w_ref, g_ref, load_sem = refs[8:14]
+    csend, crecv, msend, mrecv, x_send, x_recv = refs[14:20]
+    sp_hbm, tp_hbm, cot_hbm, w_hbm, g_hbm = refs[:5]
+    pairs = [
+        (cot_hbm, cot_ref),
+        (tp_hbm, tp_ref),
+        (g_hbm, g_ref),
+        (w_hbm.at[1], w_ref.at[1]),
+        (sp_hbm, sp_ref),
+        (w_hbm.at[0], w_ref.at[0]),
+    ]
+    loads = [pltpu.make_async_copy(s, d, load_sem.at[i]) for i, (s, d) in enumerate(pairs)]
+    for load in loads:
+        load.start()
     dp, seq = lax.axis_index("dp"), lax.axis_index("seq")
     rows, width = cot_ref.shape
     per = rows // nseq
@@ -166,6 +178,7 @@
     c_start, c_arrive, c_finish = exchange(0, csend, crecv)
     m_start, m_arrive, m_finish = exchange(1, msend, mrecv)
 
+    loads[0].wait()
     csend[...] = fold(cot_ref[...].astype(F32), nseq).astype(BF16)
     crecv[seq] = csend[seq]
 
@@ -173,21 +186,26 @@
     at = lax.broadcasted_iota(jnp.int32, (rows, rows), 0)
     frm = lax.broadcasted_iota(jnp.int32, (rows, rows), 1)
     pick = (frm == lax.rem(at, per) * frames + lax.div(at, per)).astype(F32).astype(BF16)
+    loads[1].wait()
     ut = dot(pick, tp_ref[...], 1, 0)
     ri = lax.broadcasted_iota(jnp.int32, (HEADS * rows, rows), 0)
     ci = lax.broadcasted_iota(jnp.int32, (HEADS * rows, rows), 1)
     same = lax.rem(ri, per) == lax.rem(ci, per)
+    loads[2].wait()
+    loads[3].wait()
     g_t, g_s = g_ref[1:2, :], g_ref[0:1, :]
     st = forward(ut, g_t, w_ref, 1, same)
 
     pl.semaphore_wait(barrier, npeer if fused else npeer - 1)
     c_start()
+    loads[4].wait()
+    loads[5].wait()
     ss = forward(sp_ref[...].astype(F32), g_s, w_ref, 0, None)
     c_arrive()
 
     if fused:
-        part, arecv, bsend, brecv, gown, garecv, gbsend, gbrecv = refs[14:22]
-        a_send, a_recv, b_send, b_recv = refs[22:26]
+        part, arecv, bsend, brecv, gown, garecv, gbsend, gbrecv = refs[20:28]
+        a_send, a_recv, b_send, b_recv = refs[28:32]
         chunk = part.shape[3]
 
         def near_copy(level, src, dst):
@@ -312,6 +330,28 @@
     m_finish()
 
 
+def store_kernel(*refs):
+    n = len(refs) // 2
+    sem = refs[-1]
+    copies = [pltpu.make_async_copy(refs[i], refs[n + i], sem.at[i]) for i in range(n)]
+    for c in copies:
+        c.start()
+    for c in copies:
+        c.wait()
+
+
+def store_results(results):
+    n = len(results)
+    return pl.pallas_call(
+        store_kernel,
+        out_shape=tuple(jax.ShapeDtypeStruct(r.shape, r.dtype) for r in results),
+        in_specs=[pl.BlockSpec(memory_space=pl.ANY)] * n,
+        out_specs=(pl.BlockSpec(memory_space=pltpu.HBM),) * n,
+        scratch_shapes=[pltpu.SemaphoreType.DMA((n,))],
+        compiler_params=pltpu.CompilerParams(vmem_limit_bytes=1024 * 1024),
+    )(*results)
+
+
 def per_device(spatial_input, temporal_input, out_cotangent, weights, gains):
     ndp, nseq = lax.axis_size("dp"), lax.axis_size("seq")
     width = spatial_input.shape[-1]
@@ -323,7 +363,15 @@
     fused = ndp % 2 == 0 and chunk_rows * ndp * nseq == width and chunk_rows % 8 == 0
     nfar = ndp // 2 * nseq
     message = pltpu.VMEM((nseq, 2 * per, width // 2), BF16)
-    scratch = [message] * 4 + [pltpu.SemaphoreType.DMA((2, nseq))] * 2
+    args = (
+        spatial_input.reshape(rows, width),
+        temporal_input.reshape(rows, width),
+        out_cotangent.reshape(rows, width),
+        weights,
+        gains,
+    )
+    scratch = [pltpu.VMEM(a.shape, a.dtype) for a in args] + [pltpu.SemaphoreType.DMA((6,))]
+    scratch += [message] * 4 + [pltpu.SemaphoreType.DMA((2, nseq))] * 2
     if fused:
         block = (2 * chunk_rows, wide // 2)
         scratch += [
@@ -344,26 +392,21 @@
     else:
         wg_shape = jax.ShapeDtypeStruct((2, width, wide), BF16)
     vmem = pl.BlockSpec(memory_space=pltpu.VMEM)
-    input_grad, weight_grads, gain_grads = pl.pallas_call(
+    results = pl.pallas_call(
         partial(kernel, ndp, nseq, fused, factor),
         out_shape=(
             jax.ShapeDtypeStruct((rows, width), BF16),
             wg_shape,
             jax.ShapeDtypeStruct((2, width), F32),
         ),
-        in_specs=[vmem] * 5,
+        in_specs=[pl.BlockSpec(memory_space=pltpu.HBM)] * 5,
         out_specs=(vmem,) * 3,
         scratch_shapes=scratch,
         compiler_params=pltpu.CompilerParams(
             collective_id=0, has_side_effects=True, vmem_limit_bytes=48 * 1024 * 1024
         ),
-    )(
-        spatial_input.reshape(rows, width),
-        temporal_input.reshape(rows, width),
-        out_cotangent.reshape(rows, width),
-        weights,
-        gains,
-    )
+    )(*[pltpu.with_memory_space_constraint(a, pltpu.HBM) for a in args])
+    input_grad, weight_grads, gain_grads = store_results(results) if fused else results
     if not fused:
         grid = weight_grads.reshape(2, ndp, nseq, -1)
         over = lax.psum_scatter(grid, "seq", scatter_dimension=2, tiled=True)

time: 39.2 us -> 33.6 us (0.86)
  local copies, waits for them, and re-layouts: 5.99 us -> 0 us
  Pallas kernels: 32.2 us -> 32.9 us
    unnamed x13 -> x0, local copies, waits for them, and re-layouts: 5.99 us -> none
    pallas_call x0 -> x1, Pallas kernels: none -> 0.67 us  [store_results(): pl.pallas_call(store_kernel, out_shape=tuple((jax.ShapeDtypeStruct(r.shap...]
where the time goes in v2:
time: 33.6 us; the launch traced here: 33.5 us
  Pallas kernels  32.9 us (98%)
  between operations  0.64 us (2%)
    pallas_call x1, Pallas kernels, per_device(): pl.pallas_call(partial(kernel, ndp, nseq, fused, factor), out_shape=(jax....  32.2 us

profile of v2, /device:TPU:0, one launch (start us, length us, event | category | flops | bytes accessed | tf_op | source)
XLA Modules:
  0.0 33.5 jit_solution(15837795265908798413)
XLA Ops:
  0.6 32.2 %shard_map.76 = (bf16[64,256]{1,0:T(8,128)(2,1)S(1)}, f32[2,8192]{1,0:T(2,128)S(1)}, f32[2,256]{1,0:T(2,128)S(1)}) custom-call(bf16[64,256]{1,0:T(8,128)(2,1)} %bitcast.4, bf16[64,256]{1,0:T(8,128)(2,1)} %bitcast.5, bf16[64,256]{1,0:T(8,128)(2,1)} %bitcast.6, bf16[2,256,1024]{2,1,0:T(8,128)(2,1)} %refs_3_.1, f32[2,256]{1,0:T(2,128)} %refs_4_.1), custom_call_target="tpu_custom_call" | custom-call | tf_op jit(solution)/shard_map/pallas_call | solution.py:395
  32.8 0.7 %shard_map.77 = (bf16[64,256]{1,0:T(8,128)(2,1)}, f32[2,8192]{1,0:T(2,128)}, f32[2,256]{1,0:T(2,128)}) custom-call(bf16[64,256]{1,0:T(8,128)(2,1)S(1)} %get-tuple-element.9.refs_0_, f32[2,8192]{1,0:T(2,128)S(1)} %get-tuple-element.10.refs_1_, f32[2,256]{1,0:T(2,128)S(1)} %get-tuple-element.11.refs_2_), custom_call_target="tpu_custom_call" | custom-call | tf_op jit(solution)/shard_map/pallas_call | solution.py:345

commit v3 on v2

--- a/solution.py
+++ b/solution.py
@@ -71,19 +71,22 @@
     return dict(unit=unit, inv=inv, normed=normed, qs=qs, k=k, v=v, probs=probs, pb=pb, mixed=mixed)
 
 
-def backward_heads(cot, s, w_ref, block):
+def backward_value(cot, s, w_ref, block):
     rows, width = cot.shape
-    masks = head_masks(rows, width)
+    dmixed = dot(cot, w_ref[block, :, 3 * width :], 1, 1)
+    dms = spread(dmixed, head_masks(rows, width)).astype(BF16)
+    return dms, dot(s["pb"], dms, 0, 0).astype(BF16)
+
+
+def backward_scores(dms, s):
+    rows, width = s["k"].shape
     scale = 1.0 / math.sqrt(width // HEADS)
-    dmixed = dot(cot, w_ref[block, :, 3 * width :], 1, 1)
-    dms = spread(dmixed, masks).astype(BF16)
     dprobs = dot(dms, s["v"], 1, 1).astype(BF16).astype(F32)
     inner = jnp.sum(dprobs * s["probs"], axis=-1, keepdims=True)
     dscores = (s["probs"] * (dprobs - inner) * scale).astype(BF16)
-    dq = gather_heads(dot(dscores, s["k"], 1, 0), masks)
+    dq = gather_heads(dot(dscores, s["k"], 1, 0), head_masks(rows, width))
     dk = dot(dscores, s["qs"], 0, 0)
-    dv = dot(s["pb"], dms, 0, 0)
-    return dq.astype(BF16), dk.astype(BF16), dv.astype(BF16)
+    return dq.astype(BF16), dk.astype(BF16)
 
 
 def backward_input(dpacked, s, gain, w_ref, block):
@@ -96,11 +99,17 @@
     return du, dgain
 
 
-def weight_halves(cot, dq, dk, dv, s):
-    n = s["normed"]
-    left = dot(n, jnp.concatenate([dq, dk], axis=1), 0, 0)
-    right = jnp.concatenate([dot(n, dv, 0, 0), dot(s["mixed"], cot, 0, 0)], axis=1)
-    return left, right
+def each(n, body):
+    if n <= 9:
+        for i in range(1, n):
+            body(i)
+    else:
+        pl.loop(1, n)(body)
+
+
+def groups(ndp, nseq):
+    inner = 2 if nseq % 2 == 0 else 1
+    return inner, ndp // 2 * inner, nseq // inner
 
 
 def kernel(ndp, nseq, fused, factor, *refs):
@@ -122,29 +131,40 @@
     dp, seq = lax.axis_index("dp"), lax.axis_index("seq")
     rows, width = cot_ref.shape
     per = rows // nseq
-    nfar = ndp // 2 * nseq
+    inner, n1, n2 = groups(ndp, nseq)
     core = lax.rem(dp, 2)
     partner = (dp + 1 - 2 * core, seq)
-    me = lax.div(dp, 2) * nseq + seq
-
-    def far(i):
-        other = lax.rem(me + i, nfar)
-        x = lax.div(other, nseq)
-        return other, (2 * x + core, other - x * nseq)
+    far = lax.div(dp, 2)
+    z = lax.div(seq, inner)
+    y = seq - z * inner
+    me = (far * inner + y, z)
+
+    def peer1(i):
+        other = lax.rem(me[0] + i, n1)
+        x = lax.div(other, inner)
+        return other, (2 * x + core, z * inner + other - x * inner)
+
+    def peer2(i):
+        other = lax.rem(z + i, n2)
+        return other, (dp, other * inner + y)
 
     def near(i):
         other = lax.rem(seq + i, nseq)
         return other, (dp, other)
 
     barrier = pltpu.get_barrier_semaphore()
+
+    def greet(device):
+        pl.semaphore_signal(barrier, inc=1, device_id=device, device_id_type=MESH)
+
+    each(nseq, lambda i: greet(near(i)[1]))
+    greeted = nseq - 1
     if fused:
-        pl.semaphore_signal(barrier, inc=1, device_id=partner, device_id_type=MESH)
-
-    peer, npeer = (far, nfar) if fused else (near, nseq)
-
-    @pl.loop(1, npeer)
-    def _(i):
-        pl.semaphore_signal(barrier, inc=1, device_id=peer(i)[1], device_id_type=MESH)
+        greet(partner)
+        nx = ndp // 2
+        for k in range(inner):
+            each(nx, lambda i: greet((2 * lax.rem(far + i, nx) + core, z * inner + k)))
+        greeted += 1 + inner * (nx - 1)
 
     def exchange(level, send, recv):
         def copy(i, slot):
@@ -159,19 +179,13 @@
             )
 
         def start():
-            @pl.loop(1, nseq)
-            def _(i):
-                copy(i, lambda other: seq).start()
+            each(nseq, lambda i: copy(i, lambda other: seq).start())
 
         def arrive():
-            @pl.loop(1, nseq)
-            def _(i):
-                copy(i, lambda other: other).wait_recv()
+            each(nseq, lambda i: copy(i, lambda other: other).wait_recv())
 
         def finish():
-            @pl.loop(1, nseq)
-            def _(i):
-                copy(i, lambda other: seq).wait_send()
+            each(nseq, lambda i: copy(i, lambda other: seq).wait_send())
 
         return start, arrive, finish
 
@@ -196,7 +210,7 @@
     g_t, g_s = g_ref[1:2, :], g_ref[0:1, :]
     st = forward(ut, g_t, w_ref, 1, same)
 
-    pl.semaphore_wait(barrier, npeer if fused else npeer - 1)
+    pl.semaphore_wait(barrier, greeted)
     c_start()
     loads[4].wait()
     loads[5].wait()
@@ -204,128 +218,147 @@
     c_arrive()
 
     if fused:
-        part, arecv, bsend, brecv, gown, garecv, gbsend, gbrecv = refs[20:28]
-        a_send, a_recv, b_send, b_recv = refs[28:32]
-        chunk = part.shape[3]
-
-        def near_copy(level, src, dst):
-            return pltpu.make_async_remote_copy(
-                src_ref=src,
-                dst_ref=dst,
-                send_sem=a_send.at[level],
-                recv_sem=a_recv.at[level],
+        part, arecv, send1, recv1, send2, recv2 = refs[20:26]
+        gown, garecv, gsend1, grecv1, gsend2, grecv2 = refs[26:32]
+        a_send, a_recv, s_send1, s_recv1, s_send2, s_recv2 = refs[32:38]
+        chunk = part.shape[4]
+        sends = (send1, send2)
+        recvs = (recv1, recv2)
+        gsends = (gsend1, gsend2)
+        grecvs = (grecv1, grecv2)
+        send_sems = (s_send1, s_send2)
+        recv_sems = (s_recv1, s_recv2)
+        peers = (peer1, peer2)
+        sizes = (n1, n2)
+
+        a_copies = [
+            pltpu.make_async_remote_copy(
+                src_ref=gown if p == 4 else part.at[p, 1 - core],
+                dst_ref=garecv if p == 4 else arecv.at[p],
+                send_sem=a_send.at[p],
+                recv_sem=a_recv.at[p],
                 device_id=partner,
                 device_id_type=MESH,
             )
-
-        a_copies = [near_copy(b, part.at[b, 1 - core], arecv.at[b]) for b in range(2)]
-        a_copies.append(near_copy(2, gown, garecv))
-
-        def far_copy(level, i, sending):
-            other, device = far(i)
-            slot = me if sending else other
-            if level == 2:
-                src, dst = gbsend, gbrecv.at[slot]
-            else:
-                src, dst = bsend.at[level, other], brecv.at[level, slot]
+            for p in range(5)
+        ]
+
+        def far_copy(level, p, i, sending):
+            other, device = peers[level](i)
+            slot = me[level] if sending else other
             return pltpu.make_async_remote_copy(
-                src_ref=src,
-                dst_ref=dst,
-                send_sem=b_send.at[level, other],
-                recv_sem=b_recv.at[level, slot],
+                src_ref=gsends[level] if p == 4 else sends[level].at[p, other],
+                dst_ref=grecvs[level].at[slot] if p == 4 else recvs[level].at[p, slot],
+                send_sem=send_sems[level].at[p, other],
+                recv_sem=recv_sems[level].at[p, slot],
                 device_id=device,
                 device_id_type=MESH,
             )
 
-        def put_weights(b, left, right):
+        def put(p, top, bottom):
             both = jnp.concatenate(
-                [left.reshape(2 * nfar, chunk // 2, -1), right.reshape(2 * nfar, chunk // 2, -1)],
-                axis=1,
+                [g.reshape(ndp * nseq, chunk // 2, -1) for g in (top, bottom)], axis=1
             ).astype(BF16)
-            both = both.reshape(ndp // 2, 2, nseq, chunk, -1)
+            both = both.reshape(ndp // 2, 2, n2, inner, chunk, -1)
             for c in range(2):
-                part[b, c] = both[:, c].reshape(nfar, chunk, -1)
-            a_copies[b].start()
-
-        def far_start(b):
-            a_copies[b].wait_recv()
-            total = part[b, core].astype(F32) + arecv[b].astype(F32)
-            bsend[b] = total.astype(BF16)
-            brecv[b, me] = bsend[b, me]
-
-            @pl.loop(1, nfar)
-            def _(i):
-                far_copy(b, i, True).start()
-
-        def far_end(b):
-            @pl.loop(1, nfar)
-            def _(i):
-                far_copy(b, i, False).wait_recv()
-
-            total = jnp.sum(brecv[b].astype(F32), axis=0) * factor
-            r = chunk // 2
-            half = total.shape[1]
+                for x in range(ndp // 2):
+                    for k in range(inner):
+                        part[p, c, x * inner + k] = both[x, c, :, k]
+            a_copies[p].start()
+
+        def level1(p):
+            a_copies[p].wait_recv()
+            if p == 4:
+                gsend1[...] = gown[...] + garecv[...]
+                grecv1[me[0]] = gsend1[...]
+            else:
+                send1[p] = (part[p, core].astype(F32) + arecv[p].astype(F32)).astype(BF16)
+                recv1[p, me[0]] = send1[p, me[0]]
+            each(n1, lambda i: far_copy(0, p, i, True).start())
+
+        def level2(p):
+            each(n1, lambda i: far_copy(0, p, i, False).wait_recv())
+            if p == 4:
+                gsend2[...] = jnp.sum(grecv1[...], axis=0)
+                grecv2[me[1]] = gsend2[...]
+            else:
+                send2[p] = jnp.sum(recv1[p].astype(F32), axis=0).astype(BF16)
+                recv2[p, me[1]] = send2[p, me[1]]
+            each(n2, lambda i: far_copy(1, p, i, True).start())
+
+        def last(p):
+            each(n2, lambda i: far_copy(1, p, i, False).wait_recv())
+            if p == 4:
+                gg_ref[...] = jnp.sum(grecv2[...], axis=0)[0:2] * factor
+                return
+            total = jnp.sum(recv2[p].astype(F32), axis=0) * factor
+            r, w = chunk // 2, total.shape[1]
+            b = 1 - p // 2
             for i in range(r):
-                wg_ref[b : b + 1, 2 * i * half : (2 * i + 1) * half] = total[i : i + 1]
-                wg_ref[b : b + 1, (2 * i + 1) * half : (2 * i + 2) * half] = total[r + i : r + i + 1]
+                at = 4 * w * i + 2 * w * (1 - p % 2)
+                wg_ref[b : b + 1, at : at + w] = total[i : i + 1]
+                wg_ref[b : b + 1, at + w : at + 2 * w] = total[r + i : r + i + 1]
     else:
 
-        def put_weights(b, left, right):
-            w = left.shape[1]
-            wg_ref[b, :, :w] = (left * factor).astype(BF16)
-            wg_ref[b, :, w:] = (right * factor).astype(BF16)
+        def put(p, top, bottom):
+            at = 2 * width * (1 - p % 2)
+            b = 1 - p // 2
+            wg_ref[b, :, at : at + width] = (top * factor).astype(BF16)
+            wg_ref[b, :, at + width : at + 2 * width] = (bottom * factor).astype(BF16)
+
+        def level1(p):
+            pass
+
+        level2 = last = level1
 
     cot_t = unfold(crecv[...].astype(F32))
     cot_tb = cot_t.astype(BF16)
-    dq, dk, dv = backward_heads(cot_tb, st, w_ref, 1)
+    dms, dv = backward_value(cot_tb, st, w_ref, 1)
+    dq, dk = backward_scores(dms, st)
     du, dg_t = backward_input(jnp.concatenate([dq, dk, dv], axis=1), st, g_t, w_ref, 1)
     msend[...] = fold(cot_t + du, nseq).astype(BF16)
     mrecv[seq] = msend[seq]
     m_start()
-    put_weights(1, *weight_halves(cot_tb, dq, dk, dv, st))
+    put(0, dot(st["normed"], dv, 0, 0), dot(st["mixed"], cot_tb, 0, 0))
+    put(1, dot(st["normed"], dq, 0, 0), dot(st["normed"], dk, 0, 0))
+    level1(0)
+    level1(1)
 
     m_arrive()
     cot_s = unfold(mrecv[...].astype(F32))
     cot_sb = cot_s.astype(BF16)
-    if fused:
-        far_start(1)
-    dq, dk, dv = backward_heads(cot_sb, ss, w_ref, 0)
-    put_weights(0, *weight_halves(cot_sb, dq, dk, dv, ss))
+    dms, dv = backward_value(cot_sb, ss, w_ref, 0)
+    put(2, dot(ss["normed"], dv, 0, 0), dot(ss["mixed"], cot_sb, 0, 0))
+    level2(0)
+    level2(1)
+    dq, dk = backward_scores(dms, ss)
+    put(3, dot(ss["normed"], dq, 0, 0), dot(ss["normed"], dk, 0, 0))
+    level1(2)
     du, dg_s = backward_input(jnp.concatenate([dq, dk, dv], axis=1), ss, g_s, w_ref, 0)
-    ig_ref[...] = (cot_s + du).astype(BF16)
-
     if fused:
         gown[...] = jnp.zeros_like(gown)
         gown[0:1, :] = dg_s
         gown[1:2, :] = dg_t
-        a_copies[2].start()
-        far_start(0)
-        a_copies[2].wait_recv()
-        gbsend[...] = gown[...] + garecv[...]
-        gbrecv[me] = gbsend[...]
-
-        @pl.loop(1, nfar)
-        def _(i):
-            far_copy(2, i, True).start()
-
-        far_end(1)
-        far_end(0)
-
-        @pl.loop(1, nfar)
-        def _(i):
-            far_copy(2, i, False).wait_recv()
-
-        gg_ref[...] = jnp.sum(gbrecv[...], axis=0)[0:2] * factor
-        for c in a_copies:
-            c.wait_send()
-        for level in range(3):
-
-            @pl.loop(1, nfar)
-            def _(i):
-                far_copy(level, i, True).wait_send()
+        a_copies[4].start()
     else:
         gg_ref[0:1, :] = dg_s * factor
         gg_ref[1:2, :] = dg_t * factor
+    level1(3)
+    ig_ref[...] = (cot_s + du).astype(BF16)
+    level1(4)
+    last(0)
+    last(1)
+    level2(2)
+    level2(3)
+    level2(4)
+    last(2)
+    last(3)
+    last(4)
+    if fused:
+        for p in range(5):
+            a_copies[p].wait_send()
+            for level in range(2):
+                each(sizes[level], lambda i: far_copy(level, p, i, True).wait_send())
     c_finish()
     m_finish()
 
@@ -361,7 +394,6 @@
     wide = weights.shape[2]
     chunk_rows = width // (ndp * nseq)
     fused = ndp % 2 == 0 and chunk_rows * ndp * nseq == width and chunk_rows % 8 == 0
-    nfar = ndp // 2 * nseq
     message = pltpu.VMEM((nseq, 2 * per, width // 2), BF16)
     args = (
         spatial_input.reshape(rows, width),
@@ -373,20 +405,28 @@
     scratch = [pltpu.VMEM(a.shape, a.dtype) for a in args] + [pltpu.SemaphoreType.DMA((6,))]
     scratch += [message] * 4 + [pltpu.SemaphoreType.DMA((2, nseq))] * 2
     if fused:
-        block = (2 * chunk_rows, wide // 2)
+        _, n1, n2 = groups(ndp, nseq)
+        tile = (2 * chunk_rows, wide // 4)
+        flat = pltpu.VMEM((8, width), F32)
         scratch += [
-            pltpu.VMEM((2, 2, nfar) + block, BF16),
-            pltpu.VMEM((2, nfar) + block, BF16),
-            pltpu.VMEM((2, nfar) + block, BF16),
-            pltpu.VMEM((2, nfar) + block, BF16),
-            pltpu.VMEM((8, width), F32),
-            pltpu.VMEM((8, width), F32),
-            pltpu.VMEM((8, width), F32),
-            pltpu.VMEM((nfar, 8, width), F32),
-            pltpu.SemaphoreType.DMA((3,)),
-            pltpu.SemaphoreType.DMA((3,)),
-            pltpu.SemaphoreType.DMA((3, nfar)),
-            pltpu.SemaphoreType.DMA((3, nfar)),
+            pltpu.VMEM((4, 2, n1, n2) + tile, BF16),
+            pltpu.VMEM((4, n1, n2) + tile, BF16),
+            pltpu.VMEM((4, n1, n2) + tile, BF16),
+            pltpu.VMEM((4, n1, n2) + tile, BF16),
+            pltpu.VMEM((4, n2) + tile, BF16),
+            pltpu.VMEM((4, n2) + tile, BF16),
+            flat,
+            flat,
+            flat,
+            pltpu.VMEM((n1, 8, width), F32),
+            flat,
+            pltpu.VMEM((n2, 8, width), F32),
+            pltpu.SemaphoreType.DMA((5,)),
+            pltpu.SemaphoreType.DMA((5,)),
+            pltpu.SemaphoreType.DMA((5, n1)),
+            pltpu.SemaphoreType.DMA((5, n1)),
+            pltpu.SemaphoreType.DMA((5, n2)),
+            pltpu.SemaphoreType.DMA((5, n2)),
         ]
         wg_shape = jax.ShapeDtypeStruct((2, chunk_rows * wide), F32)
     else:

time: 33.6 us -> 29 us (0.86)
  Pallas kernels: 32.9 us -> 28.2 us
    pallas_call x1, Pallas kernels: 32.2 us -> 27.6 us  [per_device(): pl.pallas_call(partial(kernel, ndp, nseq, fused, factor), out_shape=(jax....]
where the time goes in v3:
time: 29 us; the launch traced here: 28.9 us
  Pallas kernels  28.2 us (97%)
  between operations  0.64 us (2%)
    pallas_call x1, Pallas kernels, per_device(): pl.pallas_call(partial(kernel, ndp, nseq, fused, factor), out_shape=(jax....  27.6 us
    pallas_call x1, Pallas kernels, store_results(): pl.pallas_call(store_kernel, out_shape=tuple((jax.ShapeDtypeStruct(r.shap...  0.67 us

profile of v3, /device:TPU:0, one launch (start us, length us, event | category | flops | bytes accessed | tf_op | source)
XLA Modules:
  0.0 28.9 jit_solution(14635921724033375394)
XLA Ops:
  0.6 27.6 %shard_map.76 = (bf16[64,256]{1,0:T(8,128)(2,1)S(1)}, f32[2,8192]{1,0:T(2,128)S(1)}, f32[2,256]{1,0:T(2,128)S(1)}) custom-call(bf16[64,256]{1,0:T(8,128)(2,1)} %bitcast.4, bf16[64,256]{1,0:T(8,128)(2,1)} %bitcast.5, bf16[64,256]{1,0:T(8,128)(2,1)} %bitcast.6, bf16[2,256,1024]{2,1,0:T(8,128)(2,1)} %refs_3_.1, f32[2,256]{1,0:T(2,128)} %refs_4_.1), custom_call_target="tpu_custom_call" | custom-call | tf_op jit(solution)/shard_map/pallas_call | solution.py:435
  28.2 0.7 %shard_map.77 = (bf16[64,256]{1,0:T(8,128)(2,1)}, f32[2,8192]{1,0:T(2,128)}, f32[2,256]{1,0:T(2,128)}) custom-call(bf16[64,256]{1,0:T(8,128)(2,1)S(1)} %get-tuple-element.9.refs_0_, f32[2,8192]{1,0:T(2,128)S(1)} %get-tuple-element.10.refs_1_, f32[2,256]{1,0:T(2,128)S(1)} %get-tuple-element.11.refs_2_), custom_call_target="tpu_custom_call" | custom-call | tf_op jit(solution)/shard_map/pallas_call | solution.py:378

commit v4 on v3

--- a/solution.py
+++ b/solution.py
@@ -329,8 +329,6 @@
     cot_sb = cot_s.astype(BF16)
     dms, dv = backward_value(cot_sb, ss, w_ref, 0)
     put(2, dot(ss["normed"], dv, 0, 0), dot(ss["mixed"], cot_sb, 0, 0))
-    level2(0)
-    level2(1)
     dq, dk = backward_scores(dms, ss)
     put(3, dot(ss["normed"], dq, 0, 0), dot(ss["normed"], dk, 0, 0))
     level1(2)
@@ -344,13 +342,15 @@
         gg_ref[0:1, :] = dg_s * factor
         gg_ref[1:2, :] = dg_t * factor
     level1(3)
+    level1(4)
+    level2(0)
+    level2(1)
     ig_ref[...] = (cot_s + du).astype(BF16)
-    level1(4)
-    last(0)
-    last(1)
     level2(2)
     level2(3)
     level2(4)
+    last(0)
+    last(1)
     last(2)
     last(3)
     last(4)

time: 29 us -> 28 us (0.966)
  Pallas kernels: 28.2 us -> 27.2 us
    pallas_call x1, Pallas kernels: 27.6 us -> 26.5 us  [per_device(): pl.pallas_call(partial(kernel, ndp, nseq, fused, factor), out_shape=(jax....]
where the time goes in v4:
time: 28 us; the launch traced here: 27.8 us
  Pallas kernels  27.2 us (97%)
  between operations  0.64 us (2%)
    pallas_call x1, Pallas kernels, per_device(): pl.pallas_call(partial(kernel, ndp, nseq, fused, factor), out_shape=(jax....  26.5 us
    pallas_call x1, Pallas kernels, store_results(): pl.pallas_call(store_kernel, out_shape=tuple((jax.ShapeDtypeStruct(r.shap...  0.67 us

profile of v4, /device:TPU:0, one launch (start us, length us, event | category | flops | bytes accessed | tf_op | source)
XLA Modules:
  0.0 27.8 jit_solution(16449942127522339826)
XLA Ops:
  0.6 26.5 %shard_map.76 = (bf16[64,256]{1,0:T(8,128)(2,1)S(1)}, f32[2,8192]{1,0:T(2,128)S(1)}, f32[2,256]{1,0:T(2,128)S(1)}) custom-call(bf16[64,256]{1,0:T(8,128)(2,1)} %bitcast.4, bf16[64,256]{1,0:T(8,128)(2,1)} %bitcast.5, bf16[64,256]{1,0:T(8,128)(2,1)} %bitcast.6, bf16[2,256,1024]{2,1,0:T(8,128)(2,1)} %refs_3_.1, f32[2,256]{1,0:T(2,128)} %refs_4_.1), custom_call_target="tpu_custom_call" | custom-call | tf_op jit(solution)/shard_map/pallas_call | solution.py:435
  27.1 0.7 %shard_map.77 = (bf16[64,256]{1,0:T(8,128)(2,1)}, f32[2,8192]{1,0:T(2,128)}, f32[2,256]{1,0:T(2,128)}) custom-call(bf16[64,256]{1,0:T(8,128)(2,1)S(1)} %get-tuple-element.9.refs_0_, f32[2,8192]{1,0:T(2,128)S(1)} %get-tuple-element.10.refs_1_, f32[2,256]{1,0:T(2,128)S(1)} %get-tuple-element.11.refs_2_), custom_call_target="tpu_custom_call" | custom-call | tf_op jit(solution)/shard_map/pallas_call | solution.py:378
